TPU v7x, 128 devices: a whole 4x4x4 slice. The times are simulated.
128 devices in a mesh: mesh: 16 (over z, x), bg: 8 (over y, core).
Axes of the slice: x: 4, y: 4, z: 4, core: 2. Of those that a mesh axis runs over, the one named last changes fastest.
Arguments:
- displacement: float32 [3, 64, 32, 128], P(None, 'mesh', 'bg'), may hold values from -0.4 to 0.4
- bg_coef: float32 [8, 2097152], P(None, ('mesh', 'bg')), may hold values from -0.3 to 0.3
- query_elem: int32 [128, 128, 136], P(('mesh', 'bg')), may hold values from 0 to 16383
- query_point: int32 [128, 128, 136], P(('mesh', 'bg')), may hold values from 0 to 6912, as said below
- query_coord: float32 [128, 128, 3, 136], P(('mesh', 'bg')), may hold values from 0 to 1
Outputs:
- new_displacement: float32 [3, 64, 32, 128], P(None, 'mesh', 'bg')
- line_coeffs: float32 [2, 5], replicated
Inputs may be any that keep to these rules, and one draw needn't show every extreme that they name: `query_point`: in each row every quadrature point 0 to 6911 of the row's device fills exactly one slot; all other slots hold 6912 and are empty. In every draw some owner's bucket is full in every row.
All inputs are finite; a program needn't handle non-finite values.
Results may differ from a plain program's by a relative error of at most 0.0003.
Values sent between devices are 32-bit elements; how exact they have to be, the bound alone decides.
No kernel may reach another device: no remote copies, remote signals or barrier semaphores. Data moves between devices by JAX's collectives and lax.ppermute only.
A program may use at most 64 MiB of HBM per device.

v0:
```python
import jax
import jax.numpy as jnp
import numpy as np
from jax import lax
from jax.sharding import PartitionSpec as P

PASSES = 2
LS_STEPS = 4
GAUSS_POINTS = np.array([0.5 - 0.5 * np.sqrt(0.6), 0.5, 0.5 + 0.5 * np.sqrt(0.6)])
GAUSS_WEIGHTS = np.array([5.0 / 18.0, 8.0 / 18.0, 5.0 / 18.0])


def extended(block, sides, width):
    for axis, dim in sides:
        count = lax.axis_size(axis)
        forward = [(i, i + 1) for i in range(count - 1)]
        forward.append((count - 1, 0))
        backward = [(target, source) for source, target in forward]
        low = lax.ppermute(
            lax.slice_in_dim(block, block.shape[dim] - width, None, axis=dim), axis, forward
        )
        high = lax.ppermute(lax.slice_in_dim(block, 0, width, axis=dim), axis, backward)
        block = jnp.concatenate([low, block, high], axis=dim)
    return block


def basis_tables(elements, periodic):
    node_count = 2 * elements if periodic else 2 * elements + 1
    values = np.zeros((node_count, 3 * elements))
    slopes = np.zeros((node_count, 3 * elements))
    points = GAUSS_POINTS
    shape_values = [
        2.0 * (points - 0.5) * (points - 1.0),
        -4.0 * points * (points - 1.0),
        2.0 * points * (points - 0.5),
    ]
    shape_slopes = [4.0 * points - 3.0, 4.0 - 8.0 * points, 4.0 * points - 1.0]
    for offset in range(3):
        node_rows = (2 * np.arange(elements) + offset) % node_count
        for gauss_index in range(3):
            columns = 3 * np.arange(elements) + gauss_index
            values[node_rows, columns] += shape_values[offset][gauss_index]
            slopes[node_rows, columns] += shape_slopes[offset][gauss_index]
    return (jnp.asarray(values, dtype=jnp.float32), jnp.asarray(slopes, dtype=jnp.float32))


def quad_weights(z_elems, y_elems, x_elems):
    along_z = jnp.asarray(np.tile(GAUSS_WEIGHTS, z_elems), dtype=jnp.float32)
    along_y = jnp.asarray(np.tile(GAUSS_WEIGHTS, y_elems), dtype=jnp.float32)
    along_x = jnp.asarray(np.tile(GAUSS_WEIGHTS, x_elems), dtype=jnp.float32)
    return along_z[:, None, None] * along_y[None, :, None] * along_x[None, None, :]


def gradients(node_field, tables):
    z_value, z_slope, y_value, y_slope, value_along_x, x_slope = tables
    highest = lax.Precision.HIGHEST
    value_z = jnp.einsum("czyx,zk->ckyx", node_field, z_value, precision=highest)
    slope_z = jnp.einsum("czyx,zk->ckyx", node_field, z_slope, precision=highest)
    value_zy = jnp.einsum("ckyx,yl->cklx", value_z, y_value, precision=highest)
    slope_y = jnp.einsum("ckyx,yl->cklx", value_z, y_slope, precision=highest)
    slope_zy = jnp.einsum("ckyx,yl->cklx", slope_z, y_value, precision=highest)
    deriv_x = jnp.einsum("cklx,xm->cklm", value_zy, x_slope, precision=highest)
    deriv_y = jnp.einsum("cklx,xm->cklm", slope_y, value_along_x, precision=highest)
    deriv_z = jnp.einsum("cklx,xm->cklm", slope_zy, value_along_x, precision=highest)
    return jnp.stack([deriv_x, deriv_y, deriv_z], axis=1)


def identity_block():
    return jnp.eye(3, dtype=jnp.float32)[:, :, None, None, None]


def gram(left_part, right_part):
    return jnp.sum(left_part[:, :, None] * right_part[:, None, :], axis=0)


def energy(node_field, tables, target_size_scale, weights):
    jacobian = gradients(node_field, tables) + identity_block()
    strain = gram(jacobian, jacobian) * target_size_scale - identity_block()
    return jnp.sum(weights * jnp.sum(strain * strain, axis=(0, 1)))


def line_terms(node_field, direction, tables, target_size_scale, weights):
    jacobian = gradients(node_field, tables) + identity_block()
    motion = gradients(direction, tables)
    strain_zero = gram(jacobian, jacobian) * target_size_scale - identity_block()
    mixed = gram(jacobian, motion)
    strain_one = (mixed + jnp.swapaxes(mixed, 0, 1)) * target_size_scale
    strain_two = gram(motion, motion) * target_size_scale

    def weighted(first_part, latter_portion):
        return jnp.sum(weights * jnp.sum(first_part * latter_portion, axis=(0, 1)))

    zero_zero = weighted(strain_zero, strain_zero)
    zero_one = weighted(strain_zero, strain_one)
    zero_two = weighted(strain_zero, strain_two)
    one_two = weighted(strain_one, strain_two)
    two_two = weighted(strain_two, strain_two)
    gauss_newton = weighted(strain_one, strain_one)
    return (
        zero_zero,
        2.0 * zero_one,
        gauss_newton + 2.0 * zero_two,
        2.0 * one_two,
        two_two,
        gauss_newton,
    )


def line_search(terms):
    const_term, linear, quadratic, cubic_term, quartic, gauss_newton = terms
    step_len = jnp.zeros((), jnp.float32)
    for search_turn in range(LS_STEPS):
        slope = linear + step_len * (
            2.0 * quadratic + step_len * (3.0 * cubic_term + step_len * 4.0 * quartic)
        )
        curvature = 2.0 * quadratic + step_len * (6.0 * cubic_term + step_len * 12.0 * quartic)
        step_len = step_len - slope / jnp.maximum(curvature, gauss_newton + 1e-06)
    return step_len


def inverse_square(coefs, coords):
    along_x = coords[:, 0]
    along_y = coords[:, 1]
    along_z = coords[:, 2]
    summed = jnp.zeros_like(along_x)
    for corner in range(8):
        weight_x = along_x if corner & 1 else 1.0 - along_x
        weight_y = along_y if corner & 2 else 1.0 - along_y
        weight_z = along_z if corner & 4 else 1.0 - along_z
        summed = summed + weight_x * weight_y * weight_z * coefs[:, corner]
    return jnp.exp(-2.0 * summed)


def gather_coefs(table, elem_ids):
    index_rows = elem_ids[:, 0, :]
    corner_rows = jnp.take(jnp.transpose(table), index_rows, axis=0)
    return jnp.moveaxis(corner_rows, 2, 1)


def answer(reply):
    return lax.all_to_all(reply, ("mesh", "bg"), split_axis=0, concat_axis=0, tiled=True)


def assemble(local_part):
    padded_z = extended(local_part, (("mesh", 1),), 1)
    partial_sum = local_part.at[:, 0].add(padded_z[:, 0]).at[:, -1].add(padded_z[:, -1])
    padded_y = extended(partial_sum, (("bg", 2),), 1)
    summed = partial_sum.at[:, :, 0].add(padded_y[:, :, 0]).at[:, :, -1].add(padded_y[:, :, -1])
    return summed


def shards(displacement, bg_coef, query_elem, query_point, query_coord):
    devices = lax.axis_size("mesh") * lax.axis_size("bg")
    z_elems = displacement.shape[1] // 2
    y_elems = displacement.shape[2] // 2
    x_elems = displacement.shape[3] // 2
    tables = (
        basis_tables(z_elems, False) + basis_tables(y_elems, False) + basis_tables(x_elems, True)
    )
    weights = quad_weights(z_elems, y_elems, x_elems)
    point_count = 27 * z_elems * y_elems * x_elems
    elem_ids = query_elem.reshape(devices, 1, -1)
    coords = query_coord.reshape(devices, 3, -1)
    fetched = answer(
        gather_coefs(
            bg_coef,
            lax.all_to_all(elem_ids, ("mesh", "bg"), split_axis=0, concat_axis=0, tiled=True),
        )
    )
    found_vals = inverse_square(fetched, coords).reshape(-1)
    target_size_scale = (
        jnp.zeros((point_count,), jnp.float32)
        .at[query_point.reshape(-1)]
        .set(found_vals, mode="drop")
    )
    target_size_scale = target_size_scale.reshape(3 * z_elems, 3 * y_elems, 3 * x_elems)

    def local_energy(values):
        return energy(values, tables, target_size_scale, weights)

    node_field = assemble(jnp.pad(displacement, ((0, 0), (0, 1), (0, 1), (0, 0))))
    history = []
    for newton_pass in range(PASSES):
        direction = -assemble(jax.grad(local_energy)(node_field))
        partial_terms = jnp.stack(
            line_terms(node_field, direction, tables, target_size_scale, weights)
        )
        totals = lax.psum(partial_terms, ("mesh", "bg"))
        step_len = line_search(totals)
        node_field = node_field + step_len * direction
        history.append(totals[:5] / (devices * z_elems * y_elems * x_elems))
    return (node_field[:, :-1, :-1], jnp.stack(history))


def solution(mesh):
    in_specs = (
        P(None, "mesh", "bg", None),
        P(None, ("mesh", "bg")),
        P(("mesh", "bg"), None, None),
        P(("mesh", "bg"), None, None),
        P(("mesh", "bg"), None, None, None),
    )
    out_specs = (P(None, "mesh", "bg", None), P())
    return jax.shard_map(shards, mesh=mesh, in_specs=in_specs, out_specs=out_specs, check_vma=False)
```

profile of v0, /device:TPU:1, one launch (start us, length us, event | category | flops | bytes accessed | tf_op | source)
XLA Modules:
  0.0 415.2 jit_solution(10419066818697922350)
XLA Ops:
  0.7 2.1 collective-permute-start
  4.4 10.7 %all-to-all-start = ((s32[128,1,136]{2,1,0:T(1,128)}), s32[128,1,136]{2,1,0:T(1,128)S(1)}, u32[]{:S(2)}, u32[]{:S(2)}) async-start(s32[128,1,136]{2,1,0:T(1,128)} %bitcast.21), calls=%async_computation | async-start | bytes 262144 | tf_op jit(solution)/shard_map/all_to_all | solution.py:167
  18.0 5.5 %collective-permute-start.1 = (f32[3,1,5,128]{3,1,2,0:T(1,128)S(1)}, f32[3,1,5,128]{3,1,2,0:T(1,128)S(1)}, u32[]{:S(2)}, u32[]{:S(2)}) collective-permute-start(f32[3,1,5,128]{3,1,2,0:T(1,128)S(1)} %get-tuple-element.209), channel_id=1, source_target_pairs={{8,0},{16,8},{24,16},{32,24},{40,32},{48,40},{56,48},{64,56},{72,6... | collective-permute-start | bytes 23048 | tf_op jit(solution)/shard_map/ppermute | solution.py:22
  24.3 2.4 collective-permute-start.2
  27.5 2.4 collective-permute-start.3
  29.9 5.3 %copy.167 = f32[8,16384]{0,1:T(8,128)} copy(f32[8,16384]{1,0:T(8,128)S(1)} %copy-done.4) | data formatting | bytes 1048576 | tf_op args[1]
  37.8 61.3 %gather_fusion = f32[17408,8]{1,0:T(8,128)} fusion(f32[16384,8]{1,0:T(8,128)} %bitcast.265, s32[17408]{0:T(1024)S(1)} %broadcast_clamp_fusion), kind=kCustom, calls=%fused_computation | custom fusion | bytes 1183744 | tf_op jit(solution)/shard_map/jit(_take)/gather | solution.py:136
  99.1 6.7 %copy.168 = f32[128,136,8]{1,2,0:T(8,128)S(1)} copy(f32[128,136,8]{2,1,0:T(8,128)} %bitcast.266) | data formatting | bytes 1114112 | tf_op jit(solution)/shard_map/jit(_take)/gather | solution.py:136
  107.2 7.9 %all-to-all-start.1 = ((f32[128,8,136]{2,1,0:T(8,128)}), f32[128,8,136]{2,1,0:T(8,128)S(1)}, u32[]{:S(2)}, u32[]{:S(2)}) async-start(f32[128,8,136]{2,1,0:T(8,128)} %select_bitcast_fusion), calls=%async_computation.1 | async-start | bytes 2097152 | tf_op jit(solution)/shard_map/all_to_all | solution.py:141
  116.3 17.6 %all-to-all-done.1 = f32[128,8,136]{2,1,0:T(8,128)S(1)} async-done(((f32[128,8,136]{2,1,0:T(8,128)}), f32[128,8,136]{2,1,0:T(8,128)S(1)}, u32[]{:S(2)}, u32[]{:S(2)}) %all-to-all-start.1) | async-done | bytes 557088 | tf_op jit(solution)/shard_map/all_to_all | solution.py:141
  133.9 2.9 slice_reduce_fusion.6
  137.9 64.3 %scatter_custom_fusion = f32[6912]{0:T(1024)S(1)} fusion(s32[17408]{0:T(1024)} %bitcast.268, f32[17408]{0:T(1024)S(1)} %multiply_exponential_fusion, f32[]{:T(128)} %constant.313.clone.1), kind=kCustom, calls=%fused_computation.166 | custom fusion | bytes 28160 | tf_op jit(solution)/shard_map/scatter | solution.py:174
  205.6 5.3 %collective-permute-done.4 = f32[3,1,5,128]{3,1,2,0:T(1,128)S(1)} collective-permute-done((f32[3,1,5,128]{3,1,2,0:T(1,128)S(1)}, f32[3,1,5,128]{3,1,2,0:T(1,128)S(1)}, u32[]{:S(2)}, u32[]{:S(2)}) %collective-permute-start.4) | collective-permute-done | bytes 7712 | tf_op jit(solution)/shard_map/ppermute | solution.py:19
  211.1 2.4 collective-permute-done.5
  213.7 3.6 collective-permute-start.6
  218.1 3.5 collective-permute-start.7
  228.9 2.0 stack.121
  230.9 65.5 %psum.14 = f32[6]{0:T(128)S(1)} all-reduce(f32[6]{0:T(128)S(1)} %stack.121), channel_id=1, replica_groups=mesh['mesh'=16,'bg'=8] {'mesh','bg'}, use_global_device_ids=true, to_apply=%region_18.19 | all-reduce | flops 6 | bytes 48 | tf_op jit(solution)/shard_map/psum | solution.py:188
  312.5 5.8 %collective-permute-done.8 = f32[3,1,5,128]{3,1,2,0:T(1,128)S(1)} collective-permute-done((f32[3,1,5,128]{3,1,2,0:T(1,128)S(1)}, f32[3,1,5,128]{3,1,2,0:T(1,128)S(1)}, u32[]{:S(2)}, u32[]{:S(2)}) %collective-permute-start.8) | collective-permute-done | bytes 7712 | tf_op jit(solution)/shard_map/ppermute | solution.py:19
  318.5 2.4 collective-permute-done.9
  322.8 2.2 collective-permute-done.10
  325.1 3.7 collective-permute-start.11
  336.0 2.0 stack.136
  338.0 65.3 %psum.15 = f32[6]{0:T(128)S(1)} all-reduce(f32[6]{0:T(128)S(1)} %stack.136), channel_id=1, replica_groups=mesh['mesh'=16,'bg'=8] {'mesh','bg'}, use_global_device_ids=true, to_apply=%region_36.37 | all-reduce | flops 6 | bytes 48 | tf_op jit(solution)/shard_map/psum | solution.py:188
  (157 shorter events, 35.8 us)
Async XLA Ops:
  0.6 22.8 %copy-start.7 = (f32[6]{0:T(128)S(1)}, f32[6]{0:T(128)}, u32[]{:S(2)}) copy-start(f32[6]{0:T(128)} %constant.334.clone) | copy-start | bytes 76
  0.6 26.0 %copy-start.6 = (f32[192]{0:T(256)S(1)}, f32[192]{0:T(256)}, u32[]{:S(2)}) copy-start(f32[192]{0:T(256)} %constant.335.clone) | copy-start | bytes 2308
  0.7 17.2 %copy-start.5 = (f32[3,4,4,128]{3,2,1,0:T(4,128)S(1)}, f32[3,4,4,128]{3,2,1,0:T(4,128)}, u32[]{:S(2)}) copy-start(f32[3,4,4,128]{3,2,1,0:T(4,128)} %param.38) | copy-start | bytes 73732
  0.7 29.2 %copy-start.4 = (f32[8,16384]{1,0:T(8,128)S(1)}, f32[8,16384]{1,0:T(8,128)}, u32[]{:S(2)}) copy-start(f32[8,16384]{1,0:T(8,128)} %param.39) | copy-start | bytes 1572868
  0.7 17.2 %collective-permute-start = (f32[3,1,5,128]{3,1,2,0:T(1,128)S(1)}, f32[3,1,5,128]{3,1,2,0:T(1,128)S(1)}, u32[]{:S(2)}, u32[]{:S(2)}) collective-permute-start(f32[3,1,5,128]{3,1,2,0:T(1,128)S(1)} %slice.391), channel_id=1, source_target_pairs={{0,8},{8,16},{16,24},{24,32},{32,40},{40,48},{48,56},{56,64},{64,7... | collective-permute-start | bytes 23048 | tf_op jit(solution)/shard_map/ppermute | solution.py:19
  4.4 32.8 %all-to-all-start = ((s32[128,1,136]{2,1,0:T(1,128)}), s32[128,1,136]{2,1,0:T(1,128)S(1)}, u32[]{:S(2)}, u32[]{:S(2)}) async-start(s32[128,1,136]{2,1,0:T(1,128)} %bitcast.21), calls=%async_computation | async-start | bytes 262144 | tf_op jit(solution)/shard_map/all_to_all | solution.py:167
  18.0 6.2 %collective-permute-start.1 = (f32[3,1,5,128]{3,1,2,0:T(1,128)S(1)}, f32[3,1,5,128]{3,1,2,0:T(1,128)S(1)}, u32[]{:S(2)}, u32[]{:S(2)}) collective-permute-start(f32[3,1,5,128]{3,1,2,0:T(1,128)S(1)} %get-tuple-element.209), channel_id=1, source_target_pairs={{8,0},{16,8},{24,16},{32,24},{40,32},{48,40},{56,48},{64,56},{72,6... | collective-permute-start | bytes 23048 | tf_op jit(solution)/shard_map/ppermute | solution.py:22
  24.3 3.2 collective-permute-start.2
  27.5 8.3 %collective-permute-start.3 = (f32[3,5,1,128]{3,1,2,0:T(8,128)S(1)}, f32[3,5,1,128]{3,1,2,0:T(8,128)S(1)}, u32[]{:S(2)}, u32[]{:S(2)}) collective-permute-start(f32[3,5,1,128]{3,1,2,0:T(8,128)S(1)} %get-tuple-element.207), channel_id=1, source_target_pairs={{1,0},{2,1},{3,2},{4,3},{5,4},{6,5},{7,6},{0,7},{9,8},{10,9},{11,1... | collective-permute-start | bytes 23048 | tf_op jit(solution)/shard_map/ppermute | solution.py:22
  29.9 6.0 %copy-start.3 = (f32[5,6,1,1]{0,1,3,2:T(8,128)S(1)}, f32[5,6,1,1]{0,1,3,2:T(8,128)}, u32[]{:S(2)}) copy-start(f32[5,6,1,1]{0,1,3,2:T(8,128)} %constant.344) | copy-start | bytes 364
  35.2 0.9 copy-start.2
  35.2 1.7 copy-start
  107.2 8.3 %copy-start.1 = (f32[128,192,1,1]{0,1,3,2:T(8,128)S(1)}, f32[128,192,1,1]{0,1,3,2:T(8,128)}, u32[]{:S(2)}) copy-start(f32[128,192,1,1]{0,1,3,2:T(8,128)} %constant.343) | copy-start | bytes 294916
  107.2 26.7 %all-to-all-start.1 = ((f32[128,8,136]{2,1,0:T(8,128)}), f32[128,8,136]{2,1,0:T(8,128)S(1)}, u32[]{:S(2)}, u32[]{:S(2)}) async-start(f32[128,8,136]{2,1,0:T(8,128)} %select_bitcast_fusion), calls=%async_computation.1 | async-start | bytes 2097152 | tf_op jit(solution)/shard_map/all_to_all | solution.py:141
  205.1 5.9 %collective-permute-start.4 = (f32[3,1,5,128]{3,1,2,0:T(1,128)S(1)}, f32[3,1,5,128]{3,1,2,0:T(1,128)S(1)}, u32[]{:S(2)}, u32[]{:S(2)}) collective-permute-start(f32[3,1,5,128]{3,1,2,0:T(1,128)S(1)} %slice.440), channel_id=1, source_target_pairs={{0,8},{8,16},{16,24},{24,32},{32,40},{40,48},{48,56},{56,64},{64,7... | collective-permute-start | bytes 23048 | tf_op jit(solution)/shard_map/ppermute | solution.py:19
  211.0 2.6 collective-permute-start.5
  213.7 4.5 %collective-permute-start.6 = (f32[3,5,1,128]{3,1,2,0:T(8,128)S(1)}, f32[3,5,1,128]{3,1,2,0:T(8,128)S(1)}, u32[]{:S(2)}, u32[]{:S(2)}) collective-permute-start(f32[3,5,1,128]{3,1,2,0:T(8,128)S(1)} %slice.443), channel_id=1, source_target_pairs={{0,1},{1,2},{2,3},{3,4},{4,5},{5,6},{6,7},{7,0},{8,9},{9,10},{10,1... | collective-permute-start | bytes 23048 | tf_op jit(solution)/shard_map/ppermute | solution.py:19
  218.1 4.3 %collective-permute-start.7 = (f32[3,5,1,128]{3,1,2,0:T(8,128)S(1)}, f32[3,5,1,128]{3,1,2,0:T(8,128)S(1)}, u32[]{:S(2)}, u32[]{:S(2)}) collective-permute-start(f32[3,5,1,128]{3,1,2,0:T(8,128)S(1)} %get-tuple-element.203), channel_id=1, source_target_pairs={{1,0},{2,1},{3,2},{4,3},{5,4},{6,5},{7,6},{0,7},{9,8},{10,9},{11,1... | collective-permute-start | bytes 23048 | tf_op jit(solution)/shard_map/ppermute | solution.py:22
  312.4 5.9 %collective-permute-start.8 = (f32[3,1,5,128]{3,1,2,0:T(1,128)S(1)}, f32[3,1,5,128]{3,1,2,0:T(1,128)S(1)}, u32[]{:S(2)}, u32[]{:S(2)}) collective-permute-start(f32[3,1,5,128]{3,1,2,0:T(1,128)S(1)} %slice.446), channel_id=1, source_target_pairs={{0,8},{8,16},{16,24},{24,32},{32,40},{40,48},{48,56},{56,64},{64,7... | collective-permute-start | bytes 23048 | tf_op jit(solution)/shard_map/ppermute | solution.py:19
  318.3 2.6 collective-permute-start.9
  321.0 4.1 collective-permute-start.10
  325.1 4.5 %collective-permute-start.11 = (f32[3,5,1,128]{3,1,2,0:T(8,128)S(1)}, f32[3,5,1,128]{3,1,2,0:T(8,128)S(1)}, u32[]{:S(2)}, u32[]{:S(2)}) collective-permute-start(f32[3,5,1,128]{3,1,2,0:T(8,128)S(1)} %get-tuple-element.199), channel_id=1, source_target_pairs={{1,0},{2,1},{3,2},{4,3},{5,4},{6,5},{7,6},{0,7},{9,8},{10,9},{11,1... | collective-permute-start | bytes 23048 | tf_op jit(solution)/shard_map/ppermute | solution.py:22
where the time goes:
time: 416 us; the launch traced here: 415 us
  local copies, waits for them, and re-layouts  153 us (37%)
  blocking collectives  131 us (31%)
  starting transfers between devices  44.3 us (11%)
  waiting for transfers between devices  39.7 us (10%)
  between operations  26.7 us (6%)
  matrix products  12.1 us (3%)
  other arithmetic  9.06 us (2%)
    psum x2, blocking collectives, shards(): totals = lax.psum(partial_terms, ('mesh', 'bg'))  131 us
    gather x2, local copies, waits for them, and re-layouts, gather_coefs(): corner_rows = jnp.take(jnp.transpose(table), index_rows, axis=0)  68 us
    scatter x1, local copies, waits for them, and re-layouts, shards(): target_size_scale = jnp.zeros((point_count,), jnp.float32).at[query_point...  64.3 us
    all_to_all x1, waiting for transfers between devices, answer(): lax.all_to_all(reply, ('mesh', 'bg'), split_axis=0, concat_axis=0, tiled=...  17.6 us
    ppermute x6, starting transfers between devices, extended(): lax.ppermute(lax.slice_in_dim(block, 0, width, axis=dim), axis, backward)  15.1 us
    ppermute x6, waiting for transfers between devices, extended(): lax.ppermute(lax.slice_in_dim(block, block.shape[dim] - width, None, axis...  15 us
    all_to_all x1, starting transfers between devices, shards(): lax.all_to_all(elem_ids, ('mesh', 'bg'), split_axis=0, concat_axis=0, til...  10.7 us
    ppermute x6, starting transfers between devices, extended(): lax.ppermute(lax.slice_in_dim(block, block.shape[dim] - width, None, axis...  10.6 us
  transfers between devices with their start and end apart: 14, of which 11 were waited for; matrix products, arithmetic and copies ran while one was open for 3% of the time, Pallas kernels for 0%

commit v1 on v0

--- a/solution.py
+++ b/solution.py
@@ -8,6 +8,7 @@
 LS_STEPS = 4
 GAUSS_POINTS = np.array([0.5 - 0.5 * np.sqrt(0.6), 0.5, 0.5 + 0.5 * np.sqrt(0.6)])
 GAUSS_WEIGHTS = np.array([5.0 / 18.0, 8.0 / 18.0, 5.0 / 18.0])
+raise_sizes = lambda mine: lax.psum(lax.psum(mine, axis_name="mesh"), axis_name="bg")
 
 
 def extended(block, sides, width):
@@ -185,7 +186,7 @@
         partial_terms = jnp.stack(
             line_terms(node_field, direction, tables, target_size_scale, weights)
         )
-        totals = lax.psum(partial_terms, ("mesh", "bg"))
+        totals = raise_sizes(partial_terms)
         step_len = line_search(totals)
         node_field = node_field + step_len * direction
         history.append(totals[:5] / (devices * z_elems * y_elems * x_elems))

time: 416 us -> 387 us (0.930)
  blocking collectives: 131 us -> 102 us
    psum x2 -> x4, blocking collectives: 131 us -> 102 us  [the longest x2 63.1 us: lax.psum(mine, axis_name='mesh')]
where the time goes in v1:
time: 387 us; the launch traced here: 386 us
  local copies, waits for them, and re-layouts  153 us (40%)
  blocking collectives  102 us (26%)
  starting transfers between devices  43.6 us (11%)
  waiting for transfers between devices  40 us (10%)
  between operations  26.7 us (7%)
  matrix products  12.1 us (3%)
  other arithmetic  9.06 us (2%)
    gather x2, local copies, waits for them, and re-layouts, gather_coefs(): corner_rows = jnp.take(jnp.transpose(table), index_rows, axis=0)  68 us
    scatter x1, local copies, waits for them, and re-layouts, shards(): target_size_scale = jnp.zeros((point_count,), jnp.float32).at[query_point...  64.3 us
    psum x2, blocking collectives, lax.psum(mine, axis_name='mesh')  63.1 us
    psum x2, blocking collectives, lax.psum(lax.psum(mine, axis_name='mesh'), axis_name='bg')  39.4 us
    all_to_all x1, waiting for transfers between devices, answer(): lax.all_to_all(reply, ('mesh', 'bg'), split_axis=0, concat_axis=0, tiled=...  17.6 us
    ppermute x6, waiting for transfers between devices, extended(): lax.ppermute(lax.slice_in_dim(block, block.shape[dim] - width, None, axis...  15.2 us
    ppermute x6, starting transfers between devices, extended(): lax.ppermute(lax.slice_in_dim(block, 0, width, axis=dim), axis, backward)  15.1 us
    all_to_all x1, starting transfers between devices, shards(): lax.all_to_all(elem_ids, ('mesh', 'bg'), split_axis=0, concat_axis=0, til...  10.7 us
  transfers between devices with their start and end apart: 14, of which 11 were waited for; matrix products, arithmetic and copies ran while one was open for 3% of the time, Pallas kernels for 0%

profile of v1, /device:TPU:1, one launch (start us, length us, event | category | flops | bytes accessed | tf_op | source)
XLA Modules:
  0.0 386.3 jit_solution(14983343973571094124)
XLA Ops:
  0.7 2.1 collective-permute-start
  4.4 10.7 %all-to-all-start = ((s32[128,1,136]{2,1,0:T(1,128)}), s32[128,1,136]{2,1,0:T(1,128)S(1)}, u32[]{:S(2)}, u32[]{:S(2)}) async-start(s32[128,1,136]{2,1,0:T(1,128)} %bitcast.21), calls=%async_computation | async-start | bytes 262144 | tf_op jit(solution)/shard_map/all_to_all | solution.py:168
  18.0 5.5 %collective-permute-start.1 = (f32[3,1,5,128]{3,1,2,0:T(1,128)S(1)}, f32[3,1,5,128]{3,1,2,0:T(1,128)S(1)}, u32[]{:S(2)}, u32[]{:S(2)}) collective-permute-start(f32[3,1,5,128]{3,1,2,0:T(1,128)S(1)} %get-tuple-element.209), channel_id=1, source_target_pairs={{8,0},{16,8},{24,16},{32,24},{40,32},{48,40},{56,48},{64,56},{72,6... | collective-permute-start | bytes 23048 | tf_op jit(solution)/shard_map/ppermute | solution.py:23
  24.3 2.4 collective-permute-start.2
  27.5 2.4 collective-permute-start.3
  29.9 5.3 %copy.167 = f32[8,16384]{0,1:T(8,128)} copy(f32[8,16384]{1,0:T(8,128)S(1)} %copy-done.4) | data formatting | bytes 1048576 | tf_op args[1]
  37.8 61.3 %gather_fusion = f32[17408,8]{1,0:T(8,128)} fusion(f32[16384,8]{1,0:T(8,128)} %bitcast.265, s32[17408]{0:T(1024)S(1)} %broadcast_clamp_fusion), kind=kCustom, calls=%fused_computation | custom fusion | bytes 1183744 | tf_op jit(solution)/shard_map/jit(_take)/gather | solution.py:137
  99.1 6.7 %copy.168 = f32[128,136,8]{1,2,0:T(8,128)S(1)} copy(f32[128,136,8]{2,1,0:T(8,128)} %bitcast.266) | data formatting | bytes 1114112 | tf_op jit(solution)/shard_map/jit(_take)/gather | solution.py:137
  107.2 7.9 %all-to-all-start.1 = ((f32[128,8,136]{2,1,0:T(8,128)}), f32[128,8,136]{2,1,0:T(8,128)S(1)}, u32[]{:S(2)}, u32[]{:S(2)}) async-start(f32[128,8,136]{2,1,0:T(8,128)} %select_bitcast_fusion), calls=%async_computation.1 | async-start | bytes 2097152 | tf_op jit(solution)/shard_map/all_to_all | solution.py:142
  116.3 17.6 %all-to-all-done.1 = f32[128,8,136]{2,1,0:T(8,128)S(1)} async-done(((f32[128,8,136]{2,1,0:T(8,128)}), f32[128,8,136]{2,1,0:T(8,128)S(1)}, u32[]{:S(2)}, u32[]{:S(2)}) %all-to-all-start.1) | async-done | bytes 557088 | tf_op jit(solution)/shard_map/all_to_all | solution.py:142
  133.9 2.9 slice_reduce_fusion.6
  137.9 64.3 %scatter_custom_fusion = f32[6912]{0:T(1024)S(1)} fusion(s32[17408]{0:T(1024)} %bitcast.268, f32[17408]{0:T(1024)S(1)} %multiply_exponential_fusion, f32[]{:T(128)} %constant.313.clone.1), kind=kCustom, calls=%fused_computation.166 | custom fusion | bytes 28160 | tf_op jit(solution)/shard_map/scatter | solution.py:175
  205.6 5.3 %collective-permute-done.4 = f32[3,1,5,128]{3,1,2,0:T(1,128)S(1)} collective-permute-done((f32[3,1,5,128]{3,1,2,0:T(1,128)S(1)}, f32[3,1,5,128]{3,1,2,0:T(1,128)S(1)}, u32[]{:S(2)}, u32[]{:S(2)}) %collective-permute-start.4) | collective-permute-done | bytes 7712 | tf_op jit(solution)/shard_map/ppermute | solution.py:20
  211.1 2.4 collective-permute-done.5
  213.7 3.6 collective-permute-start.6
  218.1 3.5 collective-permute-start.7
  230.9 31.5 %psum.28 = f32[6]{0:T(128)S(1)} all-reduce(f32[6]{0:T(128)S(1)} %stack.121), channel_id=1, replica_groups=mesh['mesh'=16,'bg'=8] {'mesh'}, use_global_device_ids=true, to_apply=%region_18.19 | all-reduce | flops 6 | bytes 48 | tf_op jit(solution)/shard_map/psum | solution.py:11
  262.4 19.8 %psum.29 = f32[6]{0:T(128)S(1)} all-reduce(f32[6]{0:T(128)S(1)} %psum.28), channel_id=1, replica_groups=mesh['mesh'=16,'bg'=8] {'bg'}, use_global_device_ids=true, to_apply=%region_19.20 | all-reduce | flops 6 | bytes 48 | tf_op jit(solution)/shard_map/psum | solution.py:11
  298.3 5.8 %collective-permute-done.8 = f32[3,1,5,128]{3,1,2,0:T(1,128)S(1)} collective-permute-done((f32[3,1,5,128]{3,1,2,0:T(1,128)S(1)}, f32[3,1,5,128]{3,1,2,0:T(1,128)S(1)}, u32[]{:S(2)}, u32[]{:S(2)}) %collective-permute-start.8) | collective-permute-done | bytes 7712 | tf_op jit(solution)/shard_map/ppermute | solution.py:20
  304.3 2.4 collective-permute-done.9
  307.9 2.5 collective-permute-done.10
  310.4 3.7 collective-permute-start.11
  323.4 31.5 %psum.30 = f32[6]{0:T(128)S(1)} all-reduce(f32[6]{0:T(128)S(1)} %stack.136), channel_id=1, replica_groups=mesh['mesh'=16,'bg'=8] {'mesh'}, use_global_device_ids=true, to_apply=%region_37.38 | all-reduce | flops 6 | bytes 48 | tf_op jit(solution)/shard_map/psum | solution.py:11
  354.9 19.6 %psum.31 = f32[6]{0:T(128)S(1)} all-reduce(f32[6]{0:T(128)S(1)} %psum.30), channel_id=1, replica_groups=mesh['mesh'=16,'bg'=8] {'bg'}, use_global_device_ids=true, to_apply=%region_38.39 | all-reduce | flops 6 | bytes 48 | tf_op jit(solution)/shard_map/psum | solution.py:11
  (159 shorter events, 39.0 us)
Async XLA Ops:
  0.6 22.8 %copy-start.7 = (f32[6]{0:T(128)S(1)}, f32[6]{0:T(128)}, u32[]{:S(2)}) copy-start(f32[6]{0:T(128)} %constant.334.clone) | copy-start | bytes 76
  0.6 26.0 %copy-start.6 = (f32[192]{0:T(256)S(1)}, f32[192]{0:T(256)}, u32[]{:S(2)}) copy-start(f32[192]{0:T(256)} %constant.335.clone) | copy-start | bytes 2308
  0.7 17.2 %copy-start.5 = (f32[3,4,4,128]{3,2,1,0:T(4,128)S(1)}, f32[3,4,4,128]{3,2,1,0:T(4,128)}, u32[]{:S(2)}) copy-start(f32[3,4,4,128]{3,2,1,0:T(4,128)} %param.38) | copy-start | bytes 73732
  0.7 29.2 %copy-start.4 = (f32[8,16384]{1,0:T(8,128)S(1)}, f32[8,16384]{1,0:T(8,128)}, u32[]{:S(2)}) copy-start(f32[8,16384]{1,0:T(8,128)} %param.39) | copy-start | bytes 1572868
  0.7 17.2 %collective-permute-start = (f32[3,1,5,128]{3,1,2,0:T(1,128)S(1)}, f32[3,1,5,128]{3,1,2,0:T(1,128)S(1)}, u32[]{:S(2)}, u32[]{:S(2)}) collective-permute-start(f32[3,1,5,128]{3,1,2,0:T(1,128)S(1)} %slice.391), channel_id=1, source_target_pairs={{0,8},{8,16},{16,24},{24,32},{32,40},{40,48},{48,56},{56,64},{64,7... | collective-permute-start | bytes 23048 | tf_op jit(solution)/shard_map/ppermute | solution.py:20
  4.4 32.8 %all-to-all-start = ((s32[128,1,136]{2,1,0:T(1,128)}), s32[128,1,136]{2,1,0:T(1,128)S(1)}, u32[]{:S(2)}, u32[]{:S(2)}) async-start(s32[128,1,136]{2,1,0:T(1,128)} %bitcast.21), calls=%async_computation | async-start | bytes 262144 | tf_op jit(solution)/shard_map/all_to_all | solution.py:168
  18.0 6.2 %collective-permute-start.1 = (f32[3,1,5,128]{3,1,2,0:T(1,128)S(1)}, f32[3,1,5,128]{3,1,2,0:T(1,128)S(1)}, u32[]{:S(2)}, u32[]{:S(2)}) collective-permute-start(f32[3,1,5,128]{3,1,2,0:T(1,128)S(1)} %get-tuple-element.209), channel_id=1, source_target_pairs={{8,0},{16,8},{24,16},{32,24},{40,32},{48,40},{56,48},{64,56},{72,6... | collective-permute-start | bytes 23048 | tf_op jit(solution)/shard_map/ppermute | solution.py:23
  24.3 3.2 collective-permute-start.2
  27.5 8.3 %collective-permute-start.3 = (f32[3,5,1,128]{3,1,2,0:T(8,128)S(1)}, f32[3,5,1,128]{3,1,2,0:T(8,128)S(1)}, u32[]{:S(2)}, u32[]{:S(2)}) collective-permute-start(f32[3,5,1,128]{3,1,2,0:T(8,128)S(1)} %get-tuple-element.207), channel_id=1, source_target_pairs={{1,0},{2,1},{3,2},{4,3},{5,4},{6,5},{7,6},{0,7},{9,8},{10,9},{11,1... | collective-permute-start | bytes 23048 | tf_op jit(solution)/shard_map/ppermute | solution.py:23
  29.9 6.0 %copy-start.3 = (f32[5,6,1,1]{0,1,3,2:T(8,128)S(1)}, f32[5,6,1,1]{0,1,3,2:T(8,128)}, u32[]{:S(2)}) copy-start(f32[5,6,1,1]{0,1,3,2:T(8,128)} %constant.344) | copy-start | bytes 364
  35.2 0.9 copy-start.2
  35.2 1.7 copy-start
  107.2 8.3 %copy-start.1 = (f32[128,192,1,1]{0,1,3,2:T(8,128)S(1)}, f32[128,192,1,1]{0,1,3,2:T(8,128)}, u32[]{:S(2)}) copy-start(f32[128,192,1,1]{0,1,3,2:T(8,128)} %constant.343) | copy-start | bytes 294916
  107.2 26.7 %all-to-all-start.1 = ((f32[128,8,136]{2,1,0:T(8,128)}), f32[128,8,136]{2,1,0:T(8,128)S(1)}, u32[]{:S(2)}, u32[]{:S(2)}) async-start(f32[128,8,136]{2,1,0:T(8,128)} %select_bitcast_fusion), calls=%async_computation.1 | async-start | bytes 2097152 | tf_op jit(solution)/shard_map/all_to_all | solution.py:142
  205.1 5.9 %collective-permute-start.4 = (f32[3,1,5,128]{3,1,2,0:T(1,128)S(1)}, f32[3,1,5,128]{3,1,2,0:T(1,128)S(1)}, u32[]{:S(2)}, u32[]{:S(2)}) collective-permute-start(f32[3,1,5,128]{3,1,2,0:T(1,128)S(1)} %slice.440), channel_id=1, source_target_pairs={{0,8},{8,16},{16,24},{24,32},{32,40},{40,48},{48,56},{56,64},{64,7... | collective-permute-start | bytes 23048 | tf_op jit(solution)/shard_map/ppermute | solution.py:20
  211.0 2.6 collective-permute-start.5
  213.7 4.5 %collective-permute-start.6 = (f32[3,5,1,128]{3,1,2,0:T(8,128)S(1)}, f32[3,5,1,128]{3,1,2,0:T(8,128)S(1)}, u32[]{:S(2)}, u32[]{:S(2)}) collective-permute-start(f32[3,5,1,128]{3,1,2,0:T(8,128)S(1)} %slice.443), channel_id=1, source_target_pairs={{0,1},{1,2},{2,3},{3,4},{4,5},{5,6},{6,7},{7,0},{8,9},{9,10},{10,1... | collective-permute-start | bytes 23048 | tf_op jit(solution)/shard_map/ppermute | solution.py:20
  218.1 4.3 %collective-permute-start.7 = (f32[3,5,1,128]{3,1,2,0:T(8,128)S(1)}, f32[3,5,1,128]{3,1,2,0:T(8,128)S(1)}, u32[]{:S(2)}, u32[]{:S(2)}) collective-permute-start(f32[3,5,1,128]{3,1,2,0:T(8,128)S(1)} %get-tuple-element.203), channel_id=1, source_target_pairs={{1,0},{2,1},{3,2},{4,3},{5,4},{6,5},{7,6},{0,7},{9,8},{10,9},{11,1... | collective-permute-start | bytes 23048 | tf_op jit(solution)/shard_map/ppermute | solution.py:23
  298.3 5.9 %collective-permute-start.8 = (f32[3,1,5,128]{3,1,2,0:T(1,128)S(1)}, f32[3,1,5,128]{3,1,2,0:T(1,128)S(1)}, u32[]{:S(2)}, u32[]{:S(2)}) collective-permute-start(f32[3,1,5,128]{3,1,2,0:T(1,128)S(1)} %slice.446), channel_id=1, source_target_pairs={{0,8},{8,16},{16,24},{24,32},{32,40},{40,48},{48,56},{56,64},{64,7... | collective-permute-start | bytes 23048 | tf_op jit(solution)/shard_map/ppermute | solution.py:20
  304.2 2.6 collective-permute-start.9
  306.8 3.6 collective-permute-start.10
  310.4 4.5 %collective-permute-start.11 = (f32[3,5,1,128]{3,1,2,0:T(8,128)S(1)}, f32[3,5,1,128]{3,1,2,0:T(8,128)S(1)}, u32[]{:S(2)}, u32[]{:S(2)}) collective-permute-start(f32[3,5,1,128]{3,1,2,0:T(8,128)S(1)} %get-tuple-element.199), channel_id=1, source_target_pairs={{1,0},{2,1},{3,2},{4,3},{5,4},{6,5},{7,6},{0,7},{9,8},{10,9},{11,1... | collective-permute-start | bytes 23048 | tf_op jit(solution)/shard_map/ppermute | solution.py:23
